TPU v7x, 512 devices: a whole 4x4x16 slice. The times are simulated.
512 devices in a mesh: gy: 32 (over z, core), gx: 16 (over x, y).
Axes of the slice: x: 4, y: 4, z: 16, core: 2. Of those that a mesh axis runs over, the one named last changes fastest.
Arguments:
- level_in: bfloat16 [256, 1024, 128], P('gy', 'gx'), may hold values from -6 to 6
- w_level: bfloat16 [3, 3, 128, 128], replicated, may hold values from -0.1875 to 0.1875
- w_down: bfloat16 [2, 2, 128, 256], replicated, may hold values from -0.25 to 0.25
- w_neck: bfloat16 [3, 3, 256, 256], replicated, may hold values from -0.125 to 0.125
- cotangent: bfloat16 [128, 512, 256], P('gy', None, 'gx'), may hold values from -6 to 6
Outputs:
- neck_out: bfloat16 [128, 512, 256], P('gy', None, 'gx')
- grad_input: bfloat16 [256, 1024, 128], P('gy', 'gx')
- grad_level: bfloat16 [3, 3, 128, 128], replicated
- grad_down: bfloat16 [2, 2, 128, 256], replicated
- grad_neck: bfloat16 [3, 3, 256, 256], replicated
All inputs are finite; a program needn't handle non-finite values.
Results may differ from a plain program's by a relative error of at most 0.012.
Values may be sent and summed in bfloat16 or wider, within the bound.
A program may use at most 64 MiB of HBM per device.

v0:
```python
import math
import jax
import jax.numpy as jnp
from jax import lax
from jax.sharding import PartitionSpec as P


def extended(cells, sides, width):
    for axis, dim in sides:
        count = lax.axis_size(axis)
        ends = count - 1
        head = lax.slice_in_dim(cells, 0, width, axis=dim)
        tail = lax.slice_in_dim(cells, cells.shape[dim] - width, cells.shape[dim], axis=dim)
        cells = jnp.concatenate(
            [
                lax.ppermute(tail, axis, [(i, (i + 1) % count) for i in range(ends)]),
                cells,
                lax.ppermute(head, axis, [((i + 1) % count, i) for i in range(ends)]),
            ],
            axis=dim,
        )
    return cells


def slope_of(value):
    gate = jax.nn.sigmoid(value)
    return gate + value * gate * (1.0 - gate)


def tile_rims(field_in):
    return extended(field_in, (("gy", 0), ("gx", 1)), 1)


def conv_padded(padded, weights):
    row_count = padded.shape[0] - 2
    col_count = padded.shape[1] - 2
    result = jnp.zeros((row_count * col_count, weights.shape[3]), jnp.float32)
    for offset_y in range(3):
        for offset_x in range(3):
            window = padded[offset_y : offset_y + row_count, offset_x : offset_x + col_count]
            window = window.reshape(row_count * col_count, padded.shape[2])
            result = result + jnp.dot(
                window, weights[offset_y, offset_x], preferred_element_type=jnp.float32
            )
    return result


def weight_terms(padded, grads):
    row_count = grads.shape[0]
    col_count = grads.shape[1]
    flat_grads = grads.reshape(row_count * col_count, grads.shape[2])
    kernel_rows = []
    for offset_y in range(3):
        kernel_row = []
        for offset_x in range(3):
            window = padded[offset_y : offset_y + row_count, offset_x : offset_x + col_count]
            window = window.reshape(row_count * col_count, padded.shape[2])
            kernel_row.append(
                lax.dot_general(
                    window, flat_grads, (((0,), (0,)), ((), ())), preferred_element_type=jnp.float32
                )
            )
        kernel_rows.append(jnp.stack(kernel_row))
    return jnp.stack(kernel_rows)


def local(level_in, w_level, w_down, w_neck, cotangent):
    tile_rows = level_in.shape[0]
    tile_cols = level_in.shape[1]
    level_width = level_in.shape[2]
    neck_width = w_neck.shape[3]
    half_rows = tile_rows // 2
    half_cols = tile_cols // 2
    level_pad = tile_rims(level_in)
    level_pre = conv_padded(level_pad, w_level)
    level_flat = level_in.reshape(tile_rows * tile_cols, level_width).astype(jnp.float32)
    level_act = (level_flat + jax.nn.silu(level_pre)).astype(jnp.bfloat16)
    level_grid = level_act.reshape(half_rows, 2, half_cols, 2, level_width)
    neck_in = jnp.einsum(
        "hpwqc,pqcd->hwd", level_grid, w_down, preferred_element_type=jnp.float32
    ).astype(jnp.bfloat16)
    neck_pad = tile_rims(neck_in)
    neck_pre = conv_padded(neck_pad, w_neck)
    neck_flat = neck_in.reshape(half_rows * half_cols, neck_width).astype(jnp.float32)
    neck_tile = (
        (neck_flat + jax.nn.silu(neck_pre))
        .astype(jnp.bfloat16)
        .reshape(half_rows, half_cols, neck_width)
    )
    neck_out = lax.all_to_all(neck_tile, "gx", split_axis=2, concat_axis=1, tiled=True)
    neck_cot = lax.all_to_all(cotangent, "gx", split_axis=1, concat_axis=2, tiled=True)
    cot_flat = neck_cot.reshape(half_rows * half_cols, neck_width).astype(jnp.float32)
    neck_gate = (
        (cot_flat * slope_of(neck_pre))
        .astype(jnp.bfloat16)
        .reshape(half_rows, half_cols, neck_width)
    )
    flip_neck = jnp.transpose(w_neck[::-1, ::-1], (0, 1, 3, 2))
    gate_pad = tile_rims(neck_gate)
    neck_back = conv_padded(gate_pad, flip_neck)
    cot_tile = neck_cot.reshape(half_rows * half_cols, neck_width).astype(jnp.float32)
    neck_grad = (
        (cot_tile + neck_back).astype(jnp.bfloat16).reshape(half_rows, half_cols, neck_width)
    )
    neck_wgrad = weight_terms(neck_pad, neck_gate)
    level_back = jnp.einsum(
        "hwd,pqcd->hpwqc", neck_grad, w_down, preferred_element_type=jnp.float32
    )
    level_back = level_back.reshape(tile_rows * tile_cols, level_width)
    down_wgrad = jnp.einsum(
        "hpwqc,hwd->pqcd", level_grid, neck_grad, preferred_element_type=jnp.float32
    )
    level_gate = (
        (level_back * slope_of(level_pre))
        .astype(jnp.bfloat16)
        .reshape(tile_rows, tile_cols, level_width)
    )
    flip_level = jnp.transpose(w_level[::-1, ::-1], (0, 1, 3, 2))
    level_gpad = tile_rims(level_gate)
    grad_input = (level_back + conv_padded(level_gpad, flip_level)).astype(jnp.bfloat16)
    grad_input = grad_input.reshape(tile_rows, tile_cols, level_width)
    level_wgrad = weight_terms(level_pad, level_gate)
    device_count = lax.axis_size("gy") * lax.axis_size("gx")
    level_count = tile_rows * tile_cols * device_count
    level_scale = 1.0 / math.sqrt(level_count)
    neck_scale = 1.0 / math.sqrt(level_count // 4)
    reduced = lax.psum((level_wgrad, down_wgrad, neck_wgrad), ("gy", "gx"))
    grad_level = (reduced[0] * level_scale).astype(jnp.bfloat16)
    grad_down = (reduced[1] * neck_scale).astype(jnp.bfloat16)
    grad_neck = (reduced[2] * neck_scale).astype(jnp.bfloat16)
    return (neck_out, grad_input, grad_level, grad_down, grad_neck)


def solution(mesh):
    return jax.shard_map(
        local,
        mesh=mesh,
        in_specs=(P("gy", "gx", None), P(), P(), P(), P("gy", None, "gx")),
        out_specs=(P("gy", None, "gx"), P("gy", "gx", None), P(), P(), P()),
        check_vma=False,
    )
```

profile of v0, /device:TPU:2, one launch (start us, length us, event | category | flops | bytes accessed | tf_op | source)
XLA Modules:
  0.0 618.8 jit_solution(6595421685957169687)
XLA Ops:
  7.2 1.3 copy.37
  8.5 1.2 reshape.213
  9.7 9.2 %all-to-all-start.1 = ((bf16[16,2,1024]{2,1,0:T(2,128)(2,1)}), bf16[16,2,1024]{2,1,0:T(2,128)(2,1)S(1)}, u32[]{:S(2)}, u32[]{:S(2)}) async-start(bf16[16,2,1024]{2,1,0:T(2,128)(2,1)} %reshape.213), calls=%async_computation.1 | async-start | bytes 131072 | tf_op jit(solution)/shard_map/all_to_all | solution.py:91
  18.9 1.3 collective-permute-start
  20.2 1.4 collective-permute-start.1
  21.8 2.1 collective-permute-done.1
  24.0 3.4 collective-permute-start.2
  27.4 4.6 collective-permute-start.3
  32.3 1.0 collective-permute-done.3
  34.7 0.9 add_convert_fusion
  36.5 1.3 collective-permute-start.5
  37.8 3.9 collective-permute-start.4
  42.5 2.7 collective-permute-start.6
  45.2 5.3 collective-permute-start.7
  52.8 0.8 convolution_add_fusion.21
  53.6 0.8 fusion.19
  54.5 1.2 reshape.214
  55.6 1.4 copy.38
  57.0 0.9 reshape.205
  57.9 1.0 copy.40
  59.6 1.9 multiply_convert_fusion.4
  63.2 0.9 convolution_bitcast_fusion.6
  64.1 0.9 convolution_bitcast_fusion.7
  65.0 0.9 convolution_bitcast_fusion.8
  65.9 0.9 convolution_bitcast_fusion.9
  66.9 1.0 copy.34
  67.9 0.9 reshape.211
  68.8 8.5 %all-to-all-start = ((bf16[16,2,1024]{2,1,0:T(2,128)(2,1)}), bf16[16,2,1024]{2,1,0:T(2,128)(2,1)S(1)}, u32[]{:S(2)}, u32[]{:S(2)}) async-start(bf16[16,2,1024]{2,1,0:T(2,128)(2,1)} %reshape.211), calls=%async_computation | async-start | bytes 131072 | tf_op jit(solution)/shard_map/all_to_all | solution.py:90
  77.3 1.3 collective-permute-start.9
  78.7 3.0 collective-permute-start.8
  81.9 0.9 copy-done.18
  82.9 1.5 pad_maximum_fusion
  84.5 3.4 collective-permute-start.10
  87.9 4.6 collective-permute-start.11
  92.7 1.1 collective-permute-done.11
  98.4 1.3 collective-permute-start.13
  99.7 5.1 collective-permute-start.12
  104.9 0.9 pad_maximum_fusion.1
  105.7 1.1 convolution_bitcast_fusion
  106.9 2.8 collective-permute-start.14
  109.7 5.3 collective-permute-start.15
  115.2 1.1 collective-permute-done.15
  117.9 0.9 fusion.4
  119.0 0.9 all_to_all.23
  119.9 486.5 %all-reduce.3.cloned.1.call-done = (f32[3,3,128,128]{3,2,1,0:T(8,128)}, f32[2,2,128,256]{3,2,1,0:T(8,128)}, f32[3,3,256,256]{3,2,1,0:T(8,128)}) async-done(((f32[3,3,128,128]{3,2,1,0:T(8,128)}, f32[2,2,128,256]{3,2,1,0:T(8,128)}, f32[3,3,256,256]{3,2,1,0:T(8,128)}), (f32[3,3,128,128]{3,2,1,0:T(8,128)}, f32[2,2,128,256]{3,2,1,0:T(8,128)}, f32[3,3,256,256]{3,2,1,0:T(8,128)})) %all-reduce.3.cloned.1.call-update) | async-done | bytes 3473424 | tf_op jit(solution)/shard_map/psum | solution.py:127
  606.4 1.9 multiply_convert_fusion.1
  608.3 0.7 multiply_convert_fusion.2
  609.1 2.9 multiply_convert_fusion
  (184 shorter events, 15.1 us)
Async XLA Ops:
  7.2 29.1 %copy-start = (bf16[2,2,128,256]{3,2,1,0:T(8,128)(2,1)S(1)}, bf16[2,2,128,256]{3,2,1,0:T(8,128)(2,1)}, u32[]{:S(2)}) copy-start(bf16[2,2,128,256]{3,2,1,0:T(8,128)(2,1)} %param.7) | copy-start | bytes 786436
  7.2 11.7 %copy-start.2 = (bf16[8,64,128]{2,1,0:T(8,128)(2,1)S(1)}, bf16[8,64,128]{2,1,0:T(8,128)(2,1)}, u32[]{:S(2)}) copy-start(bf16[8,64,128]{2,1,0:T(8,128)(2,1)} %param.5) | copy-start | bytes 393220
  7.2 14.5 %copy-start.1 = (bf16[3,3,256,256]{3,2,1,0:T(8,128)(2,1)S(1)}, bf16[3,3,256,256]{3,2,1,0:T(8,128)(2,1)}, u32[]{:S(2)}) copy-start(bf16[3,3,256,256]{3,2,1,0:T(8,128)(2,1)} %param.8) | copy-start | bytes 3538948
  9.7 44.8 %all-to-all-start.1 = ((bf16[16,2,1024]{2,1,0:T(2,128)(2,1)}), bf16[16,2,1024]{2,1,0:T(2,128)(2,1)S(1)}, u32[]{:S(2)}, u32[]{:S(2)}) async-start(bf16[16,2,1024]{2,1,0:T(2,128)(2,1)} %reshape.213), calls=%async_computation.1 | async-start | bytes 131072 | tf_op jit(solution)/shard_map/all_to_all | solution.py:91
  18.9 2.8 collective-permute-start
  20.2 11.7 %copy-start.16 = (bf16[3,3,128,128]{3,2,1,0:T(8,128)(2,1)S(1)}, bf16[3,3,128,128]{3,2,1,0:T(8,128)(2,1)}, u32[]{:S(2)}) copy-start(bf16[3,3,128,128]{3,2,1,0:T(8,128)(2,1)} %param.6) | copy-start | bytes 884740
  20.2 3.6 collective-permute-start.1
  23.9 9.9 %copy-start.3 = (bf16[8,64,128]{2,1,0:T(8,128)(2,1)}, bf16[8,64,128]{2,1,0:T(8,128)(2,1)S(1)}, u32[]{:S(2)}) copy-start(bf16[8,64,128]{2,1,0:T(8,128)(2,1)S(1)} %get-tuple-element.37) | copy-start | bytes 393220
  24.0 8.3 %collective-permute-start.2 = (bf16[10,1,128]{2,1,0:T(2,128)(2,1)S(1)}, bf16[10,1,128]{2,1,0:T(2,128)(2,1)S(1)}, u32[]{:S(2)}, u32[]{:S(2)}) collective-permute-start(bf16[10,1,128]{2,1,0:T(2,128)(2,1)S(1)} %get-tuple-element.27), channel_id=1, source_target_pairs={{0,1},{1,2},{2,3},{3,4},{4,5},{5,6},{6,7},{7,8},{8,9},{9,10},{10,1... | collective-permute-start | bytes 7688 | tf_op jit(solution)/shard_map/ppermute | solution.py:16
  27.4 5.9 collective-permute-start.3
  33.5 1.1 copy-start.38
  36.5 5.9 collective-permute-start.5
  37.8 4.7 collective-permute-start.4
  42.5 8.8 %collective-permute-start.6 = (bf16[6,1,256]{2,1,0:T(2,128)(2,1)S(1)}, bf16[6,1,256]{2,1,0:T(2,128)(2,1)S(1)}, u32[]{:S(2)}, u32[]{:S(2)}) collective-permute-start(bf16[6,1,256]{2,1,0:T(2,128)(2,1)S(1)} %get-tuple-element.58), channel_id=1, source_target_pairs={{0,1},{1,2},{2,3},{3,4},{4,5},{5,6},{6,7},{7,8},{8,9},{9,10},{10,1... | collective-permute-start | bytes 9224 | tf_op jit(solution)/shard_map/ppermute | solution.py:16
  45.2 6.6 %collective-permute-start.7 = (bf16[6,1,256]{2,1,0:T(2,128)(2,1)S(1)}, bf16[6,1,256]{2,1,0:T(2,128)(2,1)S(1)}, u32[]{:S(2)}, u32[]{:S(2)}) collective-permute-start(bf16[6,1,256]{2,1,0:T(2,128)(2,1)S(1)} %get-tuple-element.59), channel_id=1, source_target_pairs={{1,0},{2,1},{3,2},{4,3},{5,4},{6,5},{7,6},{8,7},{9,8},{10,9},{11,1... | collective-permute-start | bytes 9224 | tf_op jit(solution)/shard_map/ppermute | solution.py:18
  51.9 1.7 copy-start.23
  51.9 1.7 copy-start.25
  51.9 1.7 copy-start.27
  51.9 1.7 copy-start.29
  51.9 1.7 copy-start.31
  57.9 4.2 copy-start.32
  57.9 4.4 copy-start.41
  57.9 4.6 copy-start.30
  61.5 1.7 copy-start.28
  62.1 2.0 copy-start.26
  62.3 2.7 copy-start.22
  62.6 3.4 copy-start.24
  63.2 14.1 %copy-start.42 = (bf16[1,32,256]{2,1,0:T(8,128)(2,1)S(1)}, bf16[1,32,256]{2,1,0:T(8,128)(2,1)}, u32[]{:S(2)}) copy-start(bf16[1,32,256]{2,1,0:T(8,128)(2,1)} %get-tuple-element.63) | copy-start | bytes 49156
  68.8 12.9 %copy-start.17 = (f32[1,256,256]{2,1,0:T(8,128)S(1)}, f32[1,256,256]{2,1,0:T(8,128)}, u32[]{:S(2)}) copy-start(f32[1,256,256]{2,1,0:T(8,128)} %convolution_bitcast_fusion.6) | copy-start | bytes 786436
  68.8 49.9 %all-to-all-start = ((bf16[16,2,1024]{2,1,0:T(2,128)(2,1)}), bf16[16,2,1024]{2,1,0:T(2,128)(2,1)S(1)}, u32[]{:S(2)}, u32[]{:S(2)}) async-start(bf16[16,2,1024]{2,1,0:T(2,128)(2,1)} %reshape.211), calls=%async_computation | async-start | bytes 131072 | tf_op jit(solution)/shard_map/all_to_all | solution.py:90
  77.3 529.1 %all-reduce.3.cloned.1.call-start = ((), (), s32[]{:S(2)}) async-start(), calls=%async_computation.2 | async-start | bytes 6946816 | tf_op jit(solution)/shard_map/psum | solution.py:127
  77.3 7.1 %collective-permute-start.9 = (bf16[1,32,256]{2,1,0:T(8,128)(2,1)S(1)}, bf16[1,32,256]{2,1,0:T(8,128)(2,1)S(1)}, u32[]{:S(2)}, u32[]{:S(2)}) collective-permute-start(bf16[1,32,256]{2,1,0:T(8,128)(2,1)S(1)} %copy-done.42), channel_id=1, source_target_pairs={{16,0},{32,16},{48,32},{64,48},{80,64},{96,80},{112,96},{128,112},... | collective-permute-start | bytes 49160 | tf_op jit(solution)/shard_map/ppermute | solution.py:18
  78.7 5.8 collective-permute-start.8
  81.8 1.1 copy-start.20
  84.5 8.2 %collective-permute-start.10 = (bf16[6,1,256]{2,1,0:T(2,128)(2,1)S(1)}, bf16[6,1,256]{2,1,0:T(2,128)(2,1)S(1)}, u32[]{:S(2)}, u32[]{:S(2)}) collective-permute-start(bf16[6,1,256]{2,1,0:T(2,128)(2,1)S(1)} %get-tuple-element.54), channel_id=1, source_target_pairs={{0,1},{1,2},{2,3},{3,4},{4,5},{5,6},{6,7},{7,8},{8,9},{9,10},{10,1... | collective-permute-start | bytes 9224 | tf_op jit(solution)/shard_map/ppermute | solution.py:16
  87.9 5.9 collective-permute-start.11
  95.6 1.2 copy-start.39
  95.8 1.2 copy-start.14
  96.1 1.4 copy-start.12
  96.2 1.5 copy-start.10
  96.5 1.7 copy-start.8
  98.4 8.4 %collective-permute-start.13 = (bf16[1,64,128]{2,1,0:T(8,128)(2,1)S(1)}, bf16[1,64,128]{2,1,0:T(8,128)(2,1)S(1)}, u32[]{:S(2)}, u32[]{:S(2)}) collective-permute-start(bf16[1,64,128]{2,1,0:T(8,128)(2,1)S(1)} %get-tuple-element.32), channel_id=1, source_target_pairs={{16,0},{32,16},{48,32},{64,48},{80,64},{96,80},{112,96},{128,112},... | collective-permute-start | bytes 49160 | tf_op jit(solution)/shard_map/ppermute | solution.py:18
  99.7 6.0 copy-start.37
  99.7 7.1 %collective-permute-start.12 = (bf16[1,64,128]{2,1,0:T(8,128)(2,1)S(1)}, bf16[1,64,128]{2,1,0:T(8,128)(2,1)S(1)}, u32[]{:S(2)}, u32[]{:S(2)}) collective-permute-start(bf16[1,64,128]{2,1,0:T(8,128)(2,1)S(1)} %get-tuple-element.31), channel_id=1, source_target_pairs={{0,16},{16,32},{32,48},{48,64},{64,80},{80,96},{96,112},{112,128},... | collective-permute-start | bytes 49160 | tf_op jit(solution)/shard_map/ppermute | solution.py:16
  106.8 8.2 %copy-start.15 = (bf16[3,3,128,128]{2,3,1,0:T(8,128)(2,1)S(1)}, bf16[3,3,128,128]{2,3,1,0:T(8,128)(2,1)}, u32[]{:S(2)}) copy-start(bf16[3,3,128,128]{2,3,1,0:T(8,128)(2,1)} %reverse_bitcast_fusion.1) | copy-start | bytes 884740
  106.9 8.3 %collective-permute-start.14 = (bf16[10,1,128]{2,1,0:T(2,128)(2,1)S(1)}, bf16[10,1,128]{2,1,0:T(2,128)(2,1)S(1)}, u32[]{:S(2)}, u32[]{:S(2)}) collective-permute-start(bf16[10,1,128]{2,1,0:T(2,128)(2,1)S(1)} %get-tuple-element.22), channel_id=1, source_target_pairs={{0,1},{1,2},{2,3},{3,4},{4,5},{5,6},{6,7},{7,8},{8,9},{9,10},{10,1... | collective-permute-start | bytes 7688 | tf_op jit(solution)/shard_map/ppermute | solution.py:16
  109.7 6.6 %collective-permute-start.15 = (bf16[10,1,128]{2,1,0:T(2,128)(2,1)S(1)}, bf16[10,1,128]{2,1,0:T(2,128)(2,1)S(1)}, u32[]{:S(2)}, u32[]{:S(2)}) collective-permute-start(bf16[10,1,128]{2,1,0:T(2,128)(2,1)S(1)} %get-tuple-element.23), channel_id=1, source_target_pairs={{1,0},{2,1},{3,2},{4,3},{5,4},{6,5},{7,6},{8,7},{9,8},{10,9},{11,1... | collective-permute-start | bytes 7688 | tf_op jit(solution)/shard_map/ppermute | solution.py:18
  606.4 1.9 copy-start.35
  (14 other events, 11.8 us)
Sparse Core Ops, SparseCore 0:
  106.9 499.4 all-reduce.2
where the time goes:
time: 620 us; the launch traced here: 619 us
  waiting for transfers between devices  492 us (79%)
  starting transfers between devices  68.3 us (11%)
  matrix products  19 us (3%)
  between operations  15.2 us (2%)
  local copies, waits for them, and re-layouts  15 us (2%)
  other arithmetic  9.4 us (2%)
    psum x1, waiting for transfers between devices, local(): reduced = lax.psum((level_wgrad, down_wgrad, neck_wgrad), ('gy', 'gx'))  487 us
    ppermute x8, starting transfers between devices, extended(): lax.ppermute(tail, axis, [(i, (i + 1) % count) for i in range(ends)])  25.5 us
    ppermute x8, starting transfers between devices, extended(): lax.ppermute(head, axis, [((i + 1) % count, i) for i in range(ends)])  25 us
  transfers between devices with their start and end apart: 19, of which 7 were waited for; matrix products, arithmetic and copies ran while one was open for 3% of the time, Pallas kernels for 0%

commit v1 on v0

--- a/solution.py
+++ b/solution.py
@@ -124,7 +124,7 @@
     level_count = tile_rows * tile_cols * device_count
     level_scale = 1.0 / math.sqrt(level_count)
     neck_scale = 1.0 / math.sqrt(level_count // 4)
-    reduced = lax.psum((level_wgrad, down_wgrad, neck_wgrad), ("gy", "gx"))
+    reduced = lax.psum(lax.psum((level_wgrad, down_wgrad, neck_wgrad), "gy"), "gx")
     grad_level = (reduced[0] * level_scale).astype(jnp.bfloat16)
     grad_down = (reduced[1] * neck_scale).astype(jnp.bfloat16)
     grad_neck = (reduced[2] * neck_scale).astype(jnp.bfloat16)

time: 620 us -> 463 us (0.75)
  the two profiles are of different devices: /device:TPU:2 before, /device:TPU:1 now
where the time goes in v1:
time: 463 us; the launch traced here: 462 us
  waiting for transfers between devices  353 us (76%)
  starting transfers between devices  58.2 us (13%)
  matrix products  15.6 us (3%)
  between operations  15.3 us (3%)
  local copies, waits for them, and re-layouts  10.7 us (2%)
  other arithmetic  9.43 us (2%)
    psum x1, waiting for transfers between devices, local(): lax.psum((level_wgrad, down_wgrad, neck_wgrad), 'gy')  229 us
    psum x1, waiting for transfers between devices, local(): lax.psum(lax.psum((level_wgrad, down_wgrad, neck_wgrad), 'gy'), 'gx')  109 us
    ppermute x8, starting transfers between devices, extended(): lax.ppermute(tail, axis, [(i, (i + 1) % count) for i in range(ends)])  30.8 us
    ppermute x8, waiting for transfers between devices, extended(): lax.ppermute(head, axis, [((i + 1) % count, i) for i in range(ends)])  14.3 us
    ppermute x8, starting transfers between devices, extended(): lax.ppermute(head, axis, [((i + 1) % count, i) for i in range(ends)])  14 us
    dot_general x36, matrix products, conv_padded(): jnp.dot(window, weights[offset_y, offset_x], preferred_element_type=jnp.f...  10.3 us
  transfers between devices with their start and end apart: 20, of which 8 were waited for; matrix products, arithmetic and copies ran while one was open for 3% of the time, Pallas kernels for 0%

profile of v1, /device:TPU:1, one launch (start us, length us, event | category | flops | bytes accessed | tf_op | source)
XLA Modules:
  0.0 461.9 jit_solution(1011461500029983869)
XLA Ops:
  7.2 0.8 fusion.68
  8.0 4.9 %collective-permute-start = (bf16[1,64,128]{2,1,0:T(8,128)(2,1)S(1)}, bf16[1,64,128]{2,1,0:T(8,128)(2,1)S(1)}, u32[]{:S(2)}, u32[]{:S(2)}) collective-permute-start(bf16[1,64,128]{2,1,0:T(8,128)(2,1)S(1)} %get-tuple-element.42), channel_id=1, source_target_pairs={{0,16},{16,32},{32,48},{48,64},{64,80},{80,96},{96,112},{112,128},... | collective-permute-start | bytes 49160 | tf_op jit(solution)/shard_map/ppermute | solution.py:16
  12.9 1.2 copy.37
  14.1 1.2 reshape.213
  15.3 6.8 %all-to-all-start.1 = ((bf16[16,2,1024]{2,1,0:T(2,128)(2,1)}), bf16[16,2,1024]{2,1,0:T(2,128)(2,1)S(1)}, u32[]{:S(2)}, u32[]{:S(2)}) async-start(bf16[16,2,1024]{2,1,0:T(2,128)(2,1)} %reshape.213), calls=%async_computation.1 | async-start | bytes 131072 | tf_op jit(solution)/shard_map/all_to_all | solution.py:91
  22.1 1.9 collective-permute-start.1
  24.1 3.4 collective-permute-done.1
  27.6 3.3 collective-permute-start.2
  30.9 1.3 collective-permute-start.3
  32.5 2.7 collective-permute-done.3
  36.6 0.9 add_convert_fusion
  37.8 1.9 collective-permute-start.5
  39.7 3.6 collective-permute-start.4
  43.5 0.7 collective-permute-done.4
  44.2 3.1 collective-permute-start.6
  47.3 1.3 collective-permute-start.7
  48.6 0.6 pad_maximum_fusion.13
  49.4 2.3 collective-permute-done.7
  52.7 0.8 convolution_add_fusion.21
  53.6 0.8 fusion.19
  54.4 1.2 reshape.214
  55.5 1.4 copy.38
  56.9 0.9 reshape.205
  57.9 1.0 copy.40
  58.9 1.3 multiply_convert_fusion.4
  62.3 2.1 collective-permute-start.9
  64.4 5.5 %collective-permute-start.8 = (bf16[1,32,256]{2,1,0:T(8,128)(2,1)S(1)}, bf16[1,32,256]{2,1,0:T(8,128)(2,1)S(1)}, u32[]{:S(2)}, u32[]{:S(2)}) collective-permute-start(bf16[1,32,256]{2,1,0:T(8,128)(2,1)S(1)} %get-tuple-element.65), channel_id=1, source_target_pairs={{0,16},{16,32},{32,48},{48,64},{64,80},{80,96},{96,112},{112,128},... | collective-permute-start | bytes 49160 | tf_op jit(solution)/shard_map/ppermute | solution.py:16
  70.0 1.6 pad_maximum_fusion
  71.6 4.3 collective-permute-start.10
  76.0 1.3 collective-permute-start.11
  77.5 3.1 collective-permute-done.11
  84.1 0.2 convolution_bitcast_fusion.16
  85.3 1.1 convolution_bitcast_fusion
  86.4 0.9 pad_maximum_fusion.1
  87.3 228.8 %all-reduce.5.cloned.1.call-done = (f32[3,3,128,128]{3,2,1,0:T(8,128)}, f32[2,2,128,256]{3,2,1,0:T(8,128)}, f32[3,3,256,256]{3,2,1,0:T(8,128)}) async-done(((f32[3,3,128,128]{3,2,1,0:T(8,128)}, f32[2,2,128,256]{3,2,1,0:T(8,128)}, f32[3,3,256,256]{3,2,1,0:T(8,128)}), (f32[3,3,128,128]{3,2,1,0:T(8,128)}, f32[2,2,128,256]{3,2,1,0:T(8,128)}, f32[3,3,256,256]{3,2,1,0:T(8,128)})) %all-reduce.5.cloned.1.call-update) | async-done | bytes 3473424 | tf_op jit(solution)/shard_map/psum | solution.py:127
  316.1 2.9 collective-permute-start.13
  319.1 2.8 collective-permute-start.12
  322.1 0.9 reshape.211
  323.0 6.5 %all-to-all-start = ((bf16[16,2,1024]{2,1,0:T(2,128)(2,1)}), bf16[16,2,1024]{2,1,0:T(2,128)(2,1)S(1)}, u32[]{:S(2)}, u32[]{:S(2)}) async-start(bf16[16,2,1024]{2,1,0:T(2,128)(2,1)} %reshape.211), calls=%async_computation | async-start | bytes 131072 | tf_op jit(solution)/shard_map/all_to_all | solution.py:90
  329.6 3.3 collective-permute-start.14
  332.8 1.3 collective-permute-start.15
  334.4 2.8 collective-permute-done.15
  338.8 0.9 fusion.4
  340.0 0.9 all_to_all.23
  340.8 108.7 %all-reduce.7.cloned.1.call-done = (f32[3,3,128,128]{3,2,1,0:T(8,128)}, f32[2,2,128,256]{3,2,1,0:T(8,128)}, f32[3,3,256,256]{3,2,1,0:T(8,128)}) async-done(((f32[3,3,128,128]{3,2,1,0:T(8,128)}, f32[2,2,128,256]{3,2,1,0:T(8,128)}, f32[3,3,256,256]{3,2,1,0:T(8,128)}), (f32[3,3,128,128]{3,2,1,0:T(8,128)}, f32[2,2,128,256]{3,2,1,0:T(8,128)}, f32[3,3,256,256]{3,2,1,0:T(8,128)})) %all-reduce.7.cloned.1.call-update) | async-done | bytes 3473424 | tf_op jit(solution)/shard_map/psum | solution.py:127
  449.6 1.9 multiply_convert_fusion.1
  451.5 0.7 multiply_convert_fusion.2
  452.2 2.9 multiply_convert_fusion
  (177 shorter events, 11.9 us)
Async XLA Ops:
  7.2 30.4 %copy-start = (bf16[2,2,128,256]{3,2,1,0:T(8,128)(2,1)S(1)}, bf16[2,2,128,256]{3,2,1,0:T(8,128)(2,1)}, u32[]{:S(2)}) copy-start(bf16[2,2,128,256]{3,2,1,0:T(8,128)(2,1)} %param.7) | copy-start | bytes 786436
  7.2 20.3 %copy-start.2 = (bf16[8,64,128]{2,1,0:T(8,128)(2,1)S(1)}, bf16[8,64,128]{2,1,0:T(8,128)(2,1)}, u32[]{:S(2)}) copy-start(bf16[8,64,128]{2,1,0:T(8,128)(2,1)} %param.5) | copy-start | bytes 393220
  7.2 25.0 %copy-start.15 = (bf16[3,3,128,128]{3,2,1,0:T(8,128)(2,1)S(1)}, bf16[3,3,128,128]{3,2,1,0:T(8,128)(2,1)}, u32[]{:S(2)}) copy-start(bf16[3,3,128,128]{3,2,1,0:T(8,128)(2,1)} %param.6) | copy-start | bytes 884740
  8.0 16.0 %collective-permute-start = (bf16[1,64,128]{2,1,0:T(8,128)(2,1)S(1)}, bf16[1,64,128]{2,1,0:T(8,128)(2,1)S(1)}, u32[]{:S(2)}, u32[]{:S(2)}) collective-permute-start(bf16[1,64,128]{2,1,0:T(8,128)(2,1)S(1)} %get-tuple-element.42), channel_id=1, source_target_pairs={{0,16},{16,32},{32,48},{48,64},{64,80},{80,96},{96,112},{112,128},... | collective-permute-start | bytes 49160 | tf_op jit(solution)/shard_map/ppermute | solution.py:16
  15.3 39.1 %all-to-all-start.1 = ((bf16[16,2,1024]{2,1,0:T(2,128)(2,1)}), bf16[16,2,1024]{2,1,0:T(2,128)(2,1)S(1)}, u32[]{:S(2)}, u32[]{:S(2)}) async-start(bf16[16,2,1024]{2,1,0:T(2,128)(2,1)} %reshape.213), calls=%async_computation.1 | async-start | bytes 131072 | tf_op jit(solution)/shard_map/all_to_all | solution.py:91
  22.1 294.0 %all-reduce.5.cloned.1.call-start = ((), (), s32[]{:S(2)}) async-start(), calls=%async_computation.2 | async-start | bytes 6946816 | tf_op jit(solution)/shard_map/psum | solution.py:127
  22.1 5.4 %collective-permute-start.1 = (bf16[1,64,128]{2,1,0:T(8,128)(2,1)S(1)}, bf16[1,64,128]{2,1,0:T(8,128)(2,1)S(1)}, u32[]{:S(2)}, u32[]{:S(2)}) collective-permute-start(bf16[1,64,128]{2,1,0:T(8,128)(2,1)S(1)} %get-tuple-element.41), channel_id=1, source_target_pairs={{16,0},{32,16},{48,32},{64,48},{80,64},{96,80},{112,96},{128,112},... | collective-permute-start | bytes 49160 | tf_op jit(solution)/shard_map/ppermute | solution.py:18
  27.5 4.6 %copy-start.3 = (bf16[8,64,128]{2,1,0:T(8,128)(2,1)}, bf16[8,64,128]{2,1,0:T(8,128)(2,1)S(1)}, u32[]{:S(2)}) copy-start(bf16[8,64,128]{2,1,0:T(8,128)(2,1)S(1)} %get-tuple-element.40) | copy-start | bytes 393220
  27.6 4.9 %collective-permute-start.2 = (bf16[10,1,128]{2,1,0:T(2,128)(2,1)S(1)}, bf16[10,1,128]{2,1,0:T(2,128)(2,1)S(1)}, u32[]{:S(2)}, u32[]{:S(2)}) collective-permute-start(bf16[10,1,128]{2,1,0:T(2,128)(2,1)S(1)} %get-tuple-element.30), channel_id=1, source_target_pairs={{0,1},{1,2},{2,3},{3,4},{4,5},{5,6},{6,7},{7,8},{8,9},{9,10},{10,1... | collective-permute-start | bytes 7688 | tf_op jit(solution)/shard_map/ppermute | solution.py:16
  30.9 4.4 collective-permute-start.3
  36.6 6.8 %copy-start.1 = (bf16[3,3,256,256]{3,2,1,0:T(8,128)(2,1)S(1)}, bf16[3,3,256,256]{3,2,1,0:T(8,128)(2,1)}, u32[]{:S(2)}) copy-start(bf16[3,3,256,256]{3,2,1,0:T(8,128)(2,1)} %param.8) | copy-start | bytes 3538948
  37.6 2.1 copy-start.32
  37.8 5.7 %collective-permute-start.5 = (bf16[1,32,256]{2,1,0:T(8,128)(2,1)S(1)}, bf16[1,32,256]{2,1,0:T(8,128)(2,1)S(1)}, u32[]{:S(2)}, u32[]{:S(2)}) collective-permute-start(bf16[1,32,256]{2,1,0:T(8,128)(2,1)S(1)} %get-tuple-element.70), channel_id=1, source_target_pairs={{16,0},{32,16},{48,32},{64,48},{80,64},{96,80},{112,96},{128,112},... | collective-permute-start | bytes 49160 | tf_op jit(solution)/shard_map/ppermute | solution.py:18
  39.7 4.5 collective-permute-start.4
  44.2 5.2 %collective-permute-start.6 = (bf16[6,1,256]{2,1,0:T(2,128)(2,1)S(1)}, bf16[6,1,256]{2,1,0:T(2,128)(2,1)S(1)}, u32[]{:S(2)}, u32[]{:S(2)}) collective-permute-start(bf16[6,1,256]{2,1,0:T(2,128)(2,1)S(1)} %get-tuple-element.61), channel_id=1, source_target_pairs={{0,1},{1,2},{2,3},{3,4},{4,5},{5,6},{6,7},{7,8},{8,9},{9,10},{10,1... | collective-permute-start | bytes 9224 | tf_op jit(solution)/shard_map/ppermute | solution.py:16
  47.3 4.4 collective-permute-start.7
  51.8 1.7 copy-start.17
  51.8 1.7 copy-start.19
  51.8 1.7 copy-start.21
  51.8 1.7 copy-start.23
  51.8 1.7 copy-start.25
  51.8 1.7 copy-start.27
  57.9 2.4 copy-start.28
  57.9 2.6 copy-start.37
  57.9 2.8 copy-start.26
  58.9 2.3 copy-start.29
  58.9 2.0 copy-start.24
  60.2 1.2 copy-start.22
  60.3 1.3 copy-start.20
  60.7 1.3 copy-start.18
  62.3 9.3 %collective-permute-start.9 = (bf16[1,32,256]{2,1,0:T(8,128)(2,1)S(1)}, bf16[1,32,256]{2,1,0:T(8,128)(2,1)S(1)}, u32[]{:S(2)}, u32[]{:S(2)}) collective-permute-start(bf16[1,32,256]{2,1,0:T(8,128)(2,1)S(1)} %get-tuple-element.66), channel_id=1, source_target_pairs={{16,0},{32,16},{48,32},{64,48},{80,64},{96,80},{112,96},{128,112},... | collective-permute-start | bytes 49160 | tf_op jit(solution)/shard_map/ppermute | solution.py:18
  64.4 7.2 %collective-permute-start.8 = (bf16[1,32,256]{2,1,0:T(8,128)(2,1)S(1)}, bf16[1,32,256]{2,1,0:T(8,128)(2,1)S(1)}, u32[]{:S(2)}, u32[]{:S(2)}) collective-permute-start(bf16[1,32,256]{2,1,0:T(8,128)(2,1)S(1)} %get-tuple-element.65), channel_id=1, source_target_pairs={{0,16},{16,32},{32,48},{48,64},{64,80},{80,96},{96,112},{112,128},... | collective-permute-start | bytes 49160 | tf_op jit(solution)/shard_map/ppermute | solution.py:16
  71.6 5.9 %collective-permute-start.10 = (bf16[6,1,256]{2,1,0:T(2,128)(2,1)S(1)}, bf16[6,1,256]{2,1,0:T(2,128)(2,1)S(1)}, u32[]{:S(2)}, u32[]{:S(2)}) collective-permute-start(bf16[6,1,256]{2,1,0:T(2,128)(2,1)S(1)} %get-tuple-element.57), channel_id=1, source_target_pairs={{0,1},{1,2},{2,3},{3,4},{4,5},{5,6},{6,7},{7,8},{8,9},{9,10},{10,1... | collective-permute-start | bytes 9224 | tf_op jit(solution)/shard_map/ppermute | solution.py:16
  76.0 4.7 %collective-permute-start.11 = (bf16[6,1,256]{2,1,0:T(2,128)(2,1)S(1)}, bf16[6,1,256]{2,1,0:T(2,128)(2,1)S(1)}, u32[]{:S(2)}, u32[]{:S(2)}) collective-permute-start(bf16[6,1,256]{2,1,0:T(2,128)(2,1)S(1)} %get-tuple-element.58), channel_id=1, source_target_pairs={{1,0},{2,1},{3,2},{4,3},{5,4},{6,5},{7,6},{8,7},{9,8},{10,9},{11,1... | collective-permute-start | bytes 9224 | tf_op jit(solution)/shard_map/ppermute | solution.py:18
  82.4 1.2 copy-start.35
  82.7 1.2 copy-start.14
  82.9 1.4 copy-start.12
  82.9 1.6 copy-start.10
  83.3 1.7 copy-start.8
  83.6 1.7 copy-start.33
  87.3 362.3 %all-reduce.7.cloned.1.call-start = ((), (), s32[]{:S(2)}) async-start(), calls=%async_computation.3 | async-start | bytes 6946816 | tf_op jit(solution)/shard_map/psum | solution.py:127
  316.1 5.8 %copy-start.16 = (bf16[3,3,128,128]{3,2,1,0:T(8,128)(2,1)S(1)}, bf16[3,3,128,128]{3,2,1,0:T(8,128)(2,1)}, u32[]{:S(2)}) copy-start(bf16[3,3,128,128]{3,2,1,0:T(8,128)(2,1)} %param.6) | copy-start | bytes 884740
  316.1 13.4 %collective-permute-start.13 = (bf16[1,64,128]{2,1,0:T(8,128)(2,1)S(1)}, bf16[1,64,128]{2,1,0:T(8,128)(2,1)S(1)}, u32[]{:S(2)}, u32[]{:S(2)}) collective-permute-start(bf16[1,64,128]{2,1,0:T(8,128)(2,1)S(1)} %get-tuple-element.35), channel_id=1, source_target_pairs={{16,0},{32,16},{48,32},{64,48},{80,64},{96,80},{112,96},{128,112},... | collective-permute-start | bytes 49160 | tf_op jit(solution)/shard_map/ppermute | solution.py:18
  319.1 10.5 %collective-permute-start.12 = (bf16[1,64,128]{2,1,0:T(8,128)(2,1)S(1)}, bf16[1,64,128]{2,1,0:T(8,128)(2,1)S(1)}, u32[]{:S(2)}, u32[]{:S(2)}) collective-permute-start(bf16[1,64,128]{2,1,0:T(8,128)(2,1)S(1)} %get-tuple-element.34), channel_id=1, source_target_pairs={{0,16},{16,32},{32,48},{48,64},{64,80},{80,96},{96,112},{112,128},... | collective-permute-start | bytes 49160 | tf_op jit(solution)/shard_map/ppermute | solution.py:16
  323.0 16.7 %all-to-all-start = ((bf16[16,2,1024]{2,1,0:T(2,128)(2,1)}), bf16[16,2,1024]{2,1,0:T(2,128)(2,1)S(1)}, u32[]{:S(2)}, u32[]{:S(2)}) async-start(bf16[16,2,1024]{2,1,0:T(2,128)(2,1)} %reshape.211), calls=%async_computation | async-start | bytes 131072 | tf_op jit(solution)/shard_map/all_to_all | solution.py:90
  329.6 4.8 %collective-permute-start.14 = (bf16[10,1,128]{2,1,0:T(2,128)(2,1)S(1)}, bf16[10,1,128]{2,1,0:T(2,128)(2,1)S(1)}, u32[]{:S(2)}, u32[]{:S(2)}) collective-permute-start(bf16[10,1,128]{2,1,0:T(2,128)(2,1)S(1)} %get-tuple-element.25), channel_id=1, source_target_pairs={{0,1},{1,2},{2,3},{3,4},{4,5},{5,6},{6,7},{7,8},{8,9},{9,10},{10,1... | collective-permute-start | bytes 7688 | tf_op jit(solution)/shard_map/ppermute | solution.py:16
  332.8 4.4 collective-permute-start.15
  449.6 1.9 copy-start.31
  (10 other events, 9.0 us)
Sparse Core Ops, SparseCore 0:
  87.4 228.6 all-reduce.4
  320.3 129.2 all-reduce.6
